TPU v7x, 128 devices: a whole 4x4x4 slice. The times are simulated.
128 devices in a mesh: row: 8 (over x_lo, y), col: 16 (over x_hi, z, core).
Axes of the slice: x: 4 (x_hi: 2, x_lo: 2; x = x_hi * 2 + x_lo), y: 4, z: 4, core: 2. Of those that a mesh axis runs over, the one named last changes fastest.
Arguments:
- r_vector: bfloat16 [3072, 18432], P(('row', 'col')), may hold values from -100 to 100, as said below
- r_previous: bfloat16 [3072, 18432], P(('row', 'col')), may hold values from -100 to 100, as said below
- cycle_block: bfloat16 [18432, 18432], P('row', 'col'), may hold values from -0.046875 to 0.046875
- ladder_block: bfloat16 [48, 48, 48, 48], P(None, 'col', None, 'row'), may hold values from -0.125 to 0.125
- occ_energy: float32 [48], replicated, may hold values from -3 to -0.5
- vir_energy: float32 [384], replicated, may hold values from 0.3 to 4
- beta_previous: float32 [64], replicated, may hold values from 0.3 to 3
Outputs:
- next_vector: bfloat16 [3072, 18432], P(('row', 'col'))
- alpha_coef: float32 [64], replicated
- beta_coef: float32 [64], replicated
Inputs may be any that keep to these rules, and one draw needn't show every extreme that they name: `r_vector`: real-valued amplitudes, rough from entry to entry. `r_previous`: real-valued amplitudes, rough from entry to entry.
All inputs are finite; a program needn't handle non-finite values.
Results may differ from a plain program's by a relative error of at most 0.001.
Values may be sent and summed in bfloat16 or wider, within the bound.
A program may use at most 128 MiB of HBM per device.

v0:
```python
import jax
import jax.numpy as jnp
from jax import lax
from jax.sharding import PartitionSpec as P

O = 48
V = 384
NVEC = 64


def on_device(
    r_vector, r_previous, cycle_block, ladder_block, occ_energy, vir_energy, beta_previous
):
    n_row = lax.axis_size("row")
    n_col = lax.axis_size("col")
    local_rows = r_vector.shape[0]
    row_width = r_vector.shape[1]
    all_rows = NVEC * O
    j_part = ladder_block.shape[1]
    q_part = ladder_block.shape[3]
    column_part = lax.all_to_all(r_vector, "row", split_axis=1, concat_axis=0, tiled=True)
    shaped = column_part.reshape(n_row, 1, local_rows, column_part.shape[1])
    gathered = lax.all_gather(shaped, "col", axis=1, tiled=True)
    operand = gathered.reshape(all_rows, column_part.shape[1])
    cycle_part = jnp.dot(operand, cycle_block, preferred_element_type=jnp.float32)
    ladder_part = jnp.einsum(
        "ijpq,npqa->nija",
        ladder_block,
        operand.reshape(NVEC, O, q_part, V),
        preferred_element_type=jnp.float32,
    )
    out_width = j_part * V
    partial_value = cycle_part + ladder_part.reshape(all_rows, out_width)
    summed = lax.psum_scatter(
        partial_value.reshape(n_row, n_col, local_rows, out_width),
        "row",
        scatter_dimension=0,
        tiled=True,
    )
    sigma_rows = lax.all_to_all(summed, "col", split_axis=1, concat_axis=3, tiled=True)
    sigma_rows = sigma_rows.reshape(local_rows, row_width)
    linear_index = lax.axis_index("row") * n_col + lax.axis_index("col")
    row_ids = linear_index * local_rows + jnp.arange(local_rows, dtype=jnp.int32)
    occ_index = row_ids % O
    vec_of_row = row_ids // O
    occ_rows = jnp.sum(
        jnp.where(occ_index[:, None] == jnp.arange(O)[None, :], occ_energy[None, :], 0.0), axis=1
    )
    r_float = r_vector.astype(jnp.float32)
    prev_float = r_previous.astype(jnp.float32)
    diagonal = vir_energy[None, None, :] - occ_rows[:, None, None] - occ_energy[None, :, None]
    sigma_rows = sigma_rows + (diagonal * r_float.reshape(local_rows, O, V)).reshape(
        local_rows, row_width
    )
    member = (vec_of_row[:, None] == jnp.arange(NVEC)[None, :]).astype(jnp.float32)
    count_all = O * O * V

    def per_vector(row_sums):
        return jnp.sum(member * row_sums[:, None], axis=0)

    def per_row(coefs):
        return jnp.sum(member * coefs[None, :], axis=1)

    rs_sum, rr_sum = lax.psum(
        (
            per_vector(jnp.sum(r_float * sigma_rows, axis=1)),
            per_vector(jnp.sum(r_float * r_float, axis=1)),
        ),
        ("row", "col"),
    )
    alpha_coef = rs_sum / count_all / (rr_sum / count_all + 1e-06)
    residual_vec = (
        sigma_rows
        - per_row(alpha_coef)[:, None] * r_float
        - per_row(beta_previous)[:, None] * prev_float
    )
    norm_sum = lax.psum(per_vector(jnp.sum(residual_vec * residual_vec, axis=1)), ("row", "col"))
    beta_coef = jnp.sqrt(norm_sum / count_all + 1e-06)
    next_vector = (residual_vec / per_row(beta_coef)[:, None]).astype(jnp.bfloat16)
    return (next_vector, alpha_coef, beta_coef)


def solution(mesh):
    placed = (
        P(("row", "col"), None),
        P(("row", "col"), None),
        P("row", "col"),
        P(None, "col", None, "row"),
        P(),
        P(),
        P(),
    )
    return jax.shard_map(
        on_device,
        mesh=mesh,
        in_specs=placed,
        out_specs=(P(("row", "col"), None), P(), P()),
        check_vma=False,
    )
```

profile of v0, /device:TPU:1, one launch (start us, length us, event | category | flops | bytes accessed | tf_op | source)
XLA Modules:
  0.0 714.6 jit_solution(3815246468868575005)
XLA Ops:
  7.2 1.3 copy.67
  8.5 18.4 %all_to_all.31 = bf16[24,8,2304]{2,0,1:T(8,128)(2,1)S(1)} all-to-all(bf16[24,8,2304]{2,0,1:T(8,128)(2,1)S(1)} %bitcast.48), channel_id=1, replica_groups=mesh['row'=8,'col'=16] {'row'}, dimensions={1} | all-to-all | bytes 1769472 | tf_op jit(solution)/shard_map/all_to_all | solution.py:21
  26.9 1.1 copy.44
  28.0 99.5 %all-gather.3.cloned.1.call-done = bf16[8,384,2304]{2,0,1:T(8,128)(2,1)} async-done(((bf16[8,24,2304]{2,0,1:T(8,128)(2,1)}), bf16[8,384,2304]{2,0,1:T(8,128)(2,1)}) %all-gather.3.cloned.1.call-update) | async-done | bytes 14155792 | tf_op jit(solution)/shard_map/all_gather | solution.py:23
  127.5 15.0 %copy.45 = bf16[8,384,2304]{2,1,0:T(8,128)(2,1)} copy(bf16[8,384,2304]{2,0,1:T(8,128)(2,1)} %all-gather.3.cloned.1.call-done) | data formatting | bytes 28311552 | tf_op jit(solution)/shard_map/all_gather | solution.py:23
  142.6 28.1 %reshape_reshape.3 = bf16[64,48,6,384]{3,2,1,0:T(8,128)(2,1)} reshape(bf16[8,384,2304]{2,1,0:T(8,128)(2,1)} %copy.45) | data formatting | bytes 28311552 | tf_op jit(solution)/shard_map/reshape;reshape | solution.py:29
  170.7 13.5 %fusion.2 = f32[64,48,3,384]{3,1,2,0:T(8,128)} fusion(bf16[64,48,6,384,1]{3,2,1,0,4:T(8,128)(2,1)} %bitcast.38, bf16[48,3,48,6]{2,0,3,1:T(8,128)(2,1)S(1)} %copy-done), kind=kOutput, calls=%fused_computation.3 | convolution fusion | flops 2038431744 | bytes 28394496 | tf_op jit(solution)/shard_map/ijpq,npqa->nija/dot_general | solution.py:26
  184.2 16.5 %copy.48 = f32[64,48,3,384]{3,2,1,0:T(4,128)S(1)} copy(f32[64,48,3,384]{3,1,2,0:T(8,128)} %fusion.2) | data formatting | bytes 28311552 | tf_op jit(solution)/shard_map/ijpq,npqa->nija/transpose | solution.py:26
  200.7 6.7 copy.58
  207.4 24.9 %convolution_add_fusion = f32[3072,1152]{1,0:T(8,128)} fusion(f32[3072,1152]{1,0:T(8,128)} %bitcast.44, bf16[3072,2304]{1,0:T(8,128)(2,1)S(1)} %bitcast.37, bf16[2304,1152]{1,0:T(8,128)(2,1)} %param.9), kind=kOutput, calls=%fused_computation.2 | convolution fusion | flops 16310992896 | bytes 47775744 | tf_op jit(solution)/shard_map/dot_general | solution.py:25
  232.3 11.5 %copy.49 = f32[8,16,24,1152]{3,2,0,1:T(8,128)} copy(f32[8,16,24,1152]{3,2,1,0:T(8,128)} %bitcast.43) | data formatting | bytes 28311552 | tf_op jit(solution)/shard_map/reshape | solution.py:35
  243.8 0.6 copy-done.8
  244.4 0.6 dynamic-slice
  245.0 288.9 %all-reduce.4.cloned.1.call-done = f32[8,16,24,1152]{3,2,0,1:T(8,128)} async-done(((f32[8,16,24,1152]{3,2,0,1:T(8,128)}), f32[8,16,24,1152]{3,2,0,1:T(8,128)}) %all-reduce.4.cloned.1.call-update) | async-done | bytes 14155792
  533.9 3.4 constant_dynamic-slice_fusion
  537.4 7.5 %all-to-all-start.1 = ((f32[1,16,24,1152]{3,2,0,1:T(8,128)}), f32[1,16,24,1152]{3,2,0,1:T(8,128)}, u32[]{:S(2)}, u32[]{:S(2)}) async-start(f32[1,16,24,1152]{3,2,0,1:T(8,128)} %constant_dynamic-slice_fusion), calls=%async_computation.1 | async-start | bytes 3538944 | tf_op jit(solution)/shard_map/all_to_all | solution.py:40
  546.0 23.9 %all-to-all-done.1 = f32[1,16,24,1152]{3,2,0,1:T(8,128)} async-done(((f32[1,16,24,1152]{3,2,0,1:T(8,128)}), f32[1,16,24,1152]{3,2,0,1:T(8,128)}, u32[]{:S(2)}, u32[]{:S(2)}) %all-to-all-start.1) | async-done | bytes 1769504 | tf_op jit(solution)/shard_map/all_to_all | solution.py:40
  569.8 1.7 copy.59
  571.5 1.2 copy-done.2
  572.7 0.8 fusion.6
  573.7 64.7 %all-reduce.1 = (f32[64]{0:T(128)S(1)}, f32[64]{0:T(128)S(1)}) all-reduce(f32[64]{0:T(128)S(1)} %get-tuple-element.8, f32[64]{0:T(128)S(1)} %get-tuple-element.7), channel_id=1, replica_groups=mesh['row'=8,'col'=16] {'row','col'}, use_global_device_ids=true, to_apply=%region_7.8 | all-reduce | flops 128 | bytes 1024 | tf_op jit(solution)/shard_map/psum | solution.py:64
  638.5 3.8 multiply_reduce_fusion
  642.5 62.5 %psum.23 = f32[64]{0:T(128)S(1)} all-reduce(f32[64]{0:T(128)S(1)} %select_reduce_fusion.1), channel_id=1, replica_groups=mesh['row'=8,'col'=16] {'row','col'}, use_global_device_ids=true, to_apply=%region_12.13 | all-reduce | flops 64 | bytes 512 | tf_op jit(solution)/shard_map/psum | solution.py:77
  705.2 2.6 divide_convert_fusion
  (44 shorter events, 1.8 us)
Async XLA Ops:
  7.2 163.5 %copy-start = (bf16[48,3,48,6]{2,0,3,1:T(8,128)(2,1)S(1)}, bf16[48,3,48,6]{2,0,3,1:T(8,128)(2,1)}, u32[]{:S(2)}) copy-start(bf16[48,3,48,6]{2,0,3,1:T(8,128)(2,1)} %param.10) | copy-start | bytes 248836
  7.2 120.4 %all-gather.3.cloned.1.call-start = ((), (), s32[]{:S(2)}) async-start(), calls=%async_computation.2 | async-start | bytes 15040512 | tf_op jit(solution)/shard_map/all_gather | solution.py:23
  28.0 506.0 %all-reduce.4.cloned.1.call-start = ((), (), s32[]{:S(2)}) async-start(), calls=%async_computation.3 | async-start | bytes 28311552
  184.2 23.2 %slice-start = ((s8[14155776]{0:T(1024)(128)(4,1)}), s8[4194304]{0:T(1024)(128)(4,1)S(1)}, s32[]{:S(2)}) async-start(s8[14155776]{0:T(1024)(128)(4,1)} %bitcast.35), calls=%async_computation.4 | async-start | bytes 8388608
  184.2 23.2 %slice-start.1 = ((s8[14155776]{0:T(1024)(128)(4,1)}), s8[4194304]{0:T(1024)(128)(4,1)S(1)}, s32[]{:S(2)}) async-start(s8[14155776]{0:T(1024)(128)(4,1)} %bitcast.35), calls=%async_computation.5 | async-start | bytes 8388608
  200.7 6.7 slice-start.2
  200.7 6.7 slice-start.3
  243.8 0.7 copy-start.8
  537.4 7.6 %copy-start.5 = (f32[48]{0:T(128)S(1)}, f32[48]{0:T(128)}, u32[]{:S(2)}) copy-start(f32[48]{0:T(128)} %param.11) | copy-start | bytes 580
  537.4 7.7 %copy-start.4 = (f32[384]{0:T(512)S(1)}, f32[384]{0:T(512)}, u32[]{:S(2)}) copy-start(f32[384]{0:T(512)} %param.12) | copy-start | bytes 4612
  537.4 32.5 %all-to-all-start.1 = ((f32[1,16,24,1152]{3,2,0,1:T(8,128)}), f32[1,16,24,1152]{3,2,0,1:T(8,128)}, u32[]{:S(2)}, u32[]{:S(2)}) async-start(f32[1,16,24,1152]{3,2,0,1:T(8,128)} %constant_dynamic-slice_fusion), calls=%async_computation.1 | async-start | bytes 3538944 | tf_op jit(solution)/shard_map/all_to_all | solution.py:40
  569.8 2.9 copy-start.3
  571.5 1.2 copy-start.2
  572.7 65.6 %copy-start.6 = (f32[64]{0:T(128)S(1)}, f32[64]{0:T(128)}, u32[]{:S(2)}) copy-start(f32[64]{0:T(128)} %param.13) | copy-start | bytes 772
  638.3 4.0 copy-start.7
  638.5 69.2 %copy-start.1 = (bf16[48,3,48,6]{2,0,3,1:T(8,128)(2,1)S(1)}, bf16[48,3,48,6]{2,0,3,1:T(8,128)(2,1)}, u32[]{:S(2)}) copy-start(bf16[48,3,48,6]{2,0,3,1:T(8,128)(2,1)} %param.10) | copy-start | bytes 248836
  705.0 2.8 copy-start.9
Sparse Core Ops, SparseCore 0:
  28.1 99.4 all-gather.2
  243.9 289.9 all-reduce.3
where the time goes:
time: 716 us; the launch traced here: 715 us
  waiting for transfers between devices  412 us (58%)
  blocking collectives  146 us (20%)
  local copies, waits for them, and re-layouts  88.4 us (12%)
  matrix products  38.4 us (5%)
  between operations  14.2 us (2%)
  other arithmetic  8.04 us (1%)
  starting transfers between devices  7.61 us (1%)
    unnamed x3, waiting for transfers between devices  289 us
    all_gather x1, waiting for transfers between devices, on_device(): gathered = lax.all_gather(shaped, 'col', axis=1, tiled=True)  99.5 us
    psum x1, blocking collectives, on_device(): lax.psum((per_vector(jnp.sum(r_float * sigma_rows, axis=1)), per_vector(j...  64.7 us
    psum x1, blocking collectives, on_device(): lax.psum(per_vector(jnp.sum(residual_vec * residual_vec, axis=1)), ('row'...  62.5 us
    another operation x1, local copies, waits for them, and re-layouts, on_device(): operand.reshape(NVEC, O, q_part, V)  28.1 us
    dot_general x1, matrix products, on_device(): jnp.dot(operand, cycle_block, preferred_element_type=jnp.float32)  24.9 us
    all_to_all x1, waiting for transfers between devices, on_device(): lax.all_to_all(summed, 'col', split_axis=1, concat_axis=3, tiled=True)  23.9 us
    all_to_all x1, blocking collectives, on_device(): lax.all_to_all(r_vector, 'row', split_axis=1, concat_axis=0, tiled=True)  18.4 us
  transfers between devices with their start and end apart: 3, of which 3 were waited for; matrix products, arithmetic and copies ran while one was open for 0% of the time, Pallas kernels for 0%

commit v1 on v0

--- a/solution.py
+++ b/solution.py
@@ -20,7 +20,9 @@
     q_part = ladder_block.shape[3]
     column_part = lax.all_to_all(r_vector, "row", split_axis=1, concat_axis=0, tiled=True)
     shaped = column_part.reshape(n_row, 1, local_rows, column_part.shape[1])
-    gathered = lax.all_gather(shaped, "col", axis=1, tiled=True)
+    gathered = jnp.concatenate(
+        lax.all_to_all(jnp.stack([shaped] * lax.axis_size("col")), "col", 0, 0), axis=1
+    )
     operand = gathered.reshape(all_rows, column_part.shape[1])
     cycle_part = jnp.dot(operand, cycle_block, preferred_element_type=jnp.float32)
     ladder_part = jnp.einsum(

time: 716 us -> 779 us (1.088)
  blocking collectives: 146 us -> 313 us
  waiting for transfers between devices: 412 us -> 313 us
    all_to_all x0 -> x1, blocking collectives: none -> 167 us  [on_device(): lax.all_to_all(jnp.stack([shaped] * lax.axis_size('col')), 'col', 0, 0)]
    all_gather x1 -> x0, waiting for transfers between devices: 99.5 us -> none  [on_device(): gathered = lax.all_gather(shaped, 'col', axis=1, tiled=True)]
    all_gather x1 -> x0, local copies, waits for them, and re-layouts: 15 us -> none  [on_device(): gathered = lax.all_gather(shaped, 'col', axis=1, tiled=True)]
    unnamed x3 -> x2, waiting for transfers between devices: 289 us -> 289 us
  transfers between devices with their start and end apart: 3 -> 2, of which waited for: 3 -> 2; matrix products, arithmetic and copies ran while one was open for 0% -> 0% of each run, Pallas kernels for 0% -> 0%
where the time goes in v1:
time: 779 us; the launch traced here: 778 us
  blocking collectives  313 us (40%)
  waiting for transfers between devices  313 us (40%)
  local copies, waits for them, and re-layouts  84.4 us (11%)
  matrix products  38.4 us (5%)
  between operations  14.2 us (2%)
  other arithmetic  8.04 us (1%)
    unnamed x2, waiting for transfers between devices  289 us
    all_to_all x1, blocking collectives, on_device(): lax.all_to_all(jnp.stack([shaped] * lax.axis_size('col')), 'col', 0, 0)  167 us
    psum x1, blocking collectives, on_device(): lax.psum((per_vector(jnp.sum(r_float * sigma_rows, axis=1)), per_vector(j...  64.7 us
    psum x1, blocking collectives, on_device(): lax.psum(per_vector(jnp.sum(residual_vec * residual_vec, axis=1)), ('row'...  62.5 us
    another operation x1, local copies, waits for them, and re-layouts, on_device(): operand.reshape(NVEC, O, q_part, V)  28.1 us
    dot_general x1, matrix products, on_device(): jnp.dot(operand, cycle_block, preferred_element_type=jnp.float32)  24.9 us
    all_to_all x1, waiting for transfers between devices, on_device(): lax.all_to_all(summed, 'col', split_axis=1, concat_axis=3, tiled=True)  23.9 us
    all_to_all x1, blocking collectives, on_device(): lax.all_to_all(r_vector, 'row', split_axis=1, concat_axis=0, tiled=True)  18.4 us
  transfers between devices with their start and end apart: 2, of which 2 were waited for; matrix products, arithmetic and copies ran while one was open for 0% of the time, Pallas kernels for 0%

profile of v1, /device:TPU:1, one launch (start us, length us, event | category | flops | bytes accessed | tf_op | source)
XLA Modules:
  0.0 777.9 jit_solution(10879410886352704305)
XLA Ops:
  7.2 1.3 copy.58
  8.5 18.4 %all_to_all.36 = bf16[24,8,2304]{2,0,1:T(8,128)(2,1)S(1)} all-to-all(bf16[24,8,2304]{2,0,1:T(8,128)(2,1)S(1)} %bitcast.55), channel_id=1, replica_groups=mesh['row'=8,'col'=16] {'row'}, dimensions={1} | all-to-all | bytes 1769472 | tf_op jit(solution)/shard_map/all_to_all | solution.py:21
  26.9 6.5 stack.3
  33.4 167.1 %all_to_all.37 = bf16[16,8,1,24,2304]{4,3,1,2,0:T(8,128)(2,1)S(1)} all-to-all(bf16[16,8,1,24,2304]{4,3,1,2,0:T(8,128)(2,1)} %stack.3), channel_id=1, replica_groups=mesh['row'=8,'col'=16] {'col'}, dimensions={0} | all-to-all | bytes 28311552 | tf_op jit(solution)/shard_map/all_to_all | solution.py:24
  200.4 5.5 copy.59
  206.0 28.1 %reshape_reshape_reshape.3 = bf16[64,48,6,384]{3,2,1,0:T(8,128)(2,1)} reshape(bf16[8,16,1,24,2304]{4,3,1,0,2:T(8,128)(2,1)} %bitcast.42) | data formatting | bytes 28311552 | tf_op jit(solution)/shard_map/reshape;reshape;reshape | solution.py:31
  234.1 13.5 %fusion.2 = f32[64,48,3,384]{3,1,2,0:T(8,128)} fusion(bf16[64,48,6,384,1]{3,2,1,0,4:T(8,128)(2,1)} %bitcast.46, bf16[48,3,48,6]{2,0,3,1:T(8,128)(2,1)S(1)} %copy-done), kind=kOutput, calls=%fused_computation.3 | convolution fusion | flops 2038431744 | bytes 28394496 | tf_op jit(solution)/shard_map/ijpq,npqa->nija/dot_general | solution.py:28
  247.6 16.5 %copy.37 = f32[64,48,3,384]{3,2,1,0:T(4,128)S(1)} copy(f32[64,48,3,384]{3,1,2,0:T(8,128)} %fusion.2) | data formatting | bytes 28311552 | tf_op jit(solution)/shard_map/ijpq,npqa->nija/transpose | solution.py:28
  264.1 6.7 copy.47
  270.9 24.9 %convolution_add_fusion = f32[3072,1152]{1,0:T(8,128)} fusion(f32[3072,1152]{1,0:T(8,128)} %bitcast.52, bf16[3072,2304]{1,0:T(8,128)(2,1)S(1)} %bitcast.45, bf16[2304,1152]{1,0:T(8,128)(2,1)} %param.9), kind=kOutput, calls=%fused_computation.2 | convolution fusion | flops 16310992896 | bytes 47775744 | tf_op jit(solution)/shard_map/dot_general | solution.py:27
  295.7 11.5 %copy.38 = f32[8,16,24,1152]{3,2,0,1:T(8,128)} copy(f32[8,16,24,1152]{3,2,1,0:T(8,128)} %bitcast.51) | data formatting | bytes 28311552 | tf_op jit(solution)/shard_map/reshape | solution.py:37
  307.2 0.6 copy-done.8
  307.8 0.6 dynamic-slice
  308.4 288.7 %all-reduce.4.cloned.1.call-done = f32[8,16,24,1152]{3,2,0,1:T(8,128)} async-done(((f32[8,16,24,1152]{3,2,0,1:T(8,128)}), f32[8,16,24,1152]{3,2,0,1:T(8,128)}) %all-reduce.4.cloned.1.call-update) | async-done | bytes 14155792
  597.1 3.4 constant_dynamic-slice_fusion
  600.5 7.7 all-to-all-start.2
  609.3 23.9 %all-to-all-done.2 = f32[1,16,24,1152]{3,2,0,1:T(8,128)} async-done(((f32[1,16,24,1152]{3,2,0,1:T(8,128)}), f32[1,16,24,1152]{3,2,0,1:T(8,128)}, u32[]{:S(2)}, u32[]{:S(2)}) %all-to-all-start.2) | async-done | bytes 1769504 | tf_op jit(solution)/shard_map/all_to_all | solution.py:42
  633.1 1.7 copy.48
  634.8 1.2 copy-done.2
  636.0 0.8 fusion.6
  637.0 64.7 %all-reduce.1 = (f32[64]{0:T(128)S(1)}, f32[64]{0:T(128)S(1)}) all-reduce(f32[64]{0:T(128)S(1)} %get-tuple-element.8, f32[64]{0:T(128)S(1)} %get-tuple-element.7), channel_id=1, replica_groups=mesh['row'=8,'col'=16] {'row','col'}, use_global_device_ids=true, to_apply=%region_7.8 | all-reduce | flops 128 | bytes 1024 | tf_op jit(solution)/shard_map/psum | solution.py:66
  701.8 3.8 multiply_reduce_fusion
  705.8 62.5 %psum.23 = f32[64]{0:T(128)S(1)} all-reduce(f32[64]{0:T(128)S(1)} %select_reduce_fusion.1), channel_id=1, replica_groups=mesh['row'=8,'col'=16] {'row','col'}, use_global_device_ids=true, to_apply=%region_12.13 | all-reduce | flops 64 | bytes 512 | tf_op jit(solution)/shard_map/psum | solution.py:79
  768.5 2.6 divide_convert_fusion
  (42 shorter events, 1.7 us)
Async XLA Ops:
  7.2 226.9 %copy-start = (bf16[48,3,48,6]{2,0,3,1:T(8,128)(2,1)S(1)}, bf16[48,3,48,6]{2,0,3,1:T(8,128)(2,1)}, u32[]{:S(2)}) copy-start(bf16[48,3,48,6]{2,0,3,1:T(8,128)(2,1)} %param.10) | copy-start | bytes 248836
  7.2 589.9 %all-reduce.4.cloned.1.call-start = ((), (), s32[]{:S(2)}) async-start(), calls=%async_computation.3 | async-start | bytes 28311552
  247.6 23.2 %slice-start = ((s8[14155776]{0:T(1024)(128)(4,1)}), s8[4194304]{0:T(1024)(128)(4,1)S(1)}, s32[]{:S(2)}) async-start(s8[14155776]{0:T(1024)(128)(4,1)} %bitcast.43), calls=%async_computation.4 | async-start | bytes 8388608
  247.6 23.2 %slice-start.1 = ((s8[14155776]{0:T(1024)(128)(4,1)}), s8[4194304]{0:T(1024)(128)(4,1)S(1)}, s32[]{:S(2)}) async-start(s8[14155776]{0:T(1024)(128)(4,1)} %bitcast.43), calls=%async_computation.5 | async-start | bytes 8388608
  264.1 6.7 slice-start.2
  264.1 6.7 slice-start.3
  307.2 0.7 copy-start.8
  600.5 7.7 copy-start.5
  600.5 7.9 %copy-start.4 = (f32[384]{0:T(512)S(1)}, f32[384]{0:T(512)}, u32[]{:S(2)}) copy-start(f32[384]{0:T(512)} %param.12) | copy-start | bytes 4612
  600.5 32.6 %all-to-all-start.2 = ((f32[1,16,24,1152]{3,2,0,1:T(8,128)}), f32[1,16,24,1152]{3,2,0,1:T(8,128)}, u32[]{:S(2)}, u32[]{:S(2)}) async-start(f32[1,16,24,1152]{3,2,0,1:T(8,128)} %constant_dynamic-slice_fusion), calls=%async_computation.2 | async-start | bytes 3538944 | tf_op jit(solution)/shard_map/all_to_all | solution.py:42
  633.1 2.9 copy-start.3
  634.8 1.2 copy-start.2
  636.0 65.6 %copy-start.6 = (f32[64]{0:T(128)S(1)}, f32[64]{0:T(128)}, u32[]{:S(2)}) copy-start(f32[64]{0:T(128)} %param.13) | copy-start | bytes 772
  701.6 4.0 copy-start.7
  701.8 69.2 %copy-start.1 = (bf16[48,3,48,6]{2,0,3,1:T(8,128)(2,1)S(1)}, bf16[48,3,48,6]{2,0,3,1:T(8,128)(2,1)}, u32[]{:S(2)}) copy-start(bf16[48,3,48,6]{2,0,3,1:T(8,128)(2,1)} %param.10) | copy-start | bytes 248836
  768.3 2.8 copy-start.9
Sparse Core Ops, SparseCore 0:
  307.3 289.6 all-reduce.3
